TPU v7x, 32 devices: a whole 2x2x4 slice. The times are simulated.
32 devices in a mesh: seq: 16 (over z, y, core), head: 2 (over x).
Axes of the slice: x: 2, y: 2, z: 4, core: 2. Of those that a mesh axis runs over, the one named last changes fastest.
Arguments:
- tokens: bfloat16 [512, 2048], P('seq', 'head'), may hold values from -6 to 6
- ln1_gain: float32 [2048], replicated, may hold values from 0.1 to 1.9
- ln1_shift: float32 [2048], replicated, may hold values from -1.75 to 1.75
- ln2_gain: float32 [2048], replicated, may hold values from 0.1 to 1.9
- ln2_shift: float32 [2048], replicated, may hold values from -1.75 to 1.75
- w_qkv: bfloat16 [2048, 3, 2048], P(None, None, 'head'), may hold values from -0.125 to 0.125
- b_qkv: float32 [3, 2048], P(None, 'head'), may hold values from -3 to 3
- w_dense: bfloat16 [2048, 2048], P('head'), may hold values from -0.125 to 0.125
- b_dense: float32 [2048], P('head'), may hold values from -1.75 to 1.75
- w_up: bfloat16 [2048, 4096], P(None, 'head'), may hold values from -0.125 to 0.125
- b_up: float32 [4096], P('head'), may hold values from -3 to 3
- w_down: bfloat16 [4096, 2048], P('head'), may hold values from -0.09375 to 0.09375
- b_down: float32 [2048], P('head'), may hold values from -1.75 to 1.75
- keys_short: bfloat16 [512, 64, 2048], P('seq', None, 'head'), may hold values from -210 to 210
- values_short: bfloat16 [512, 64, 2048], P('seq', None, 'head'), may hold values from -16 to 16
- keys_long: bfloat16 [32768, 2048], P('seq', 'head'), may hold values from -210 to 210
- values_long: bfloat16 [32768, 2048], P('seq', 'head'), may hold values from -16 to 16
- lengths: int32 [512], replicated, may hold values from 16 to 8192, as said below
- slot_request: int32 [512], replicated, may hold values from 0 to 511, as said below
- piece_map: int32 [16], replicated, may hold values from 0 to 15, each once
Outputs:
- layer_out: bfloat16 [512, 2048], P('seq', 'head')
Inputs may be any that keep to these rules, and one draw needn't show every extreme that they name: `lengths`: requests 0 to 3 hold more than 4096 positions, one of them exactly 8192; every other request holds 16 to 64 positions, one of them exactly 64. `slot_request`: A permutation of the requests; slot s lies on index s // 32 of seq. The requests 32 h to 32 h + 31 are served in 8 groups of exactly 4 on as many different indices of seq. Rows 2048 b to 2048 b + 2047 of keys_long and values_long hold positions (piece_map[b] % 4) * 2048 onwards of the cache of request piece_map[b] // 4.
All inputs are finite; a program needn't handle non-finite values.
Results may differ from a plain program's by a relative error of at most 0.0095.
Values may be sent and summed in bfloat16 or wider, within the bound.
A program may use at most 192 MiB of HBM per device.

v0:
```python
import jax
import jax.numpy as jnp
from jax import lax
from jax.sharding import PartitionSpec as P

HD = 256
ROT = 64
LONGS = 4
epsilon = 1e-05
very_low = -1e30


def merged(array, axis, combine):
    everything = jax.tree.map(lambda part: lax.all_gather(part, axis), array)
    first = jax.tree.map(lambda part: part[0], everything)

    def hop(k, so_far):
        return combine(so_far, jax.tree.map(lambda part: part[k], everything))

    return lax.fori_loop(1, lax.axis_size(axis), hop, first)


def layer_norm(values, gain, shift):
    center = jnp.mean(values, axis=-1, keepdims=True)
    offset = values - center
    spread = jnp.mean(offset * offset, axis=-1, keepdims=True)
    return offset * lax.rsqrt(spread + epsilon) * gain + shift


def rotary(values, position):
    half_rot = ROT // 2
    frequency = jnp.power(10000.0, -2.0 * jnp.arange(half_rot, dtype=jnp.float32) / ROT)
    angles = position.astype(jnp.float32)[:, None] * frequency[None, :]
    cosine = jnp.cos(angles)[:, None, :]
    sine_of = jnp.sin(angles)[:, None, :]
    leading = values[..., :half_rot]
    trailing = values[..., half_rot:ROT]
    return jnp.concatenate(
        [
            leading * cosine - trailing * sine_of,
            trailing * cosine + leading * sine_of,
            values[..., ROT:],
        ],
        axis=-1,
    )


def attend(queries, key_rows, value_rows, usable):
    scores = jnp.einsum(
        "rhc,rthc->rht", queries, key_rows, preferred_element_type=jnp.float32
    ) * HD ** (-0.5)
    masked = jnp.where(usable[:, None, :], scores, very_low)
    summit = jnp.max(masked, axis=-1)
    weights = jnp.where(usable[:, None, :], jnp.exp(masked - summit[..., None]), 0.0)
    amount = jnp.sum(weights, axis=-1)
    mixed = jnp.einsum(
        "rht,rthc->rhc",
        weights.astype(jnp.bfloat16),
        value_rows,
        preferred_element_type=jnp.float32,
    )
    return (summit, amount, mixed)


def combine_partials(first_part, second_part):
    top_first, total_first, out_first = first_part
    top_second, total_second, out_second = second_part
    summit = jnp.maximum(top_first, top_second)
    scale_first = jnp.exp(top_first - summit)
    scale_second = jnp.exp(top_second - summit)
    total_both = total_first * scale_first + total_second * scale_second
    out_both = out_first * scale_first[..., None] + out_second * scale_second[..., None]
    return (summit, total_both, out_both)


def local(
    tokens,
    ln1_gain,
    ln1_shift,
    ln2_gain,
    ln2_shift,
    w_qkv,
    b_qkv,
    w_dense,
    b_dense,
    w_up,
    b_up,
    w_down,
    b_down,
    keys_short,
    values_short,
    keys_long,
    values_long,
    lengths,
    slot_request,
    piece_map,
):
    slot_rows, part_width = tokens.shape
    seq_count = lax.axis_size("seq")
    seq_place = lax.axis_index("seq")
    request_count = slot_request.shape[0]
    heads_here = part_width // HD
    my_requests = lax.dynamic_slice_in_dim(slot_request, seq_place * slot_rows, slot_rows)
    shard_rows = lax.all_gather(tokens, "seq", axis=0, tiled=True)
    row_ids = jnp.arange(shard_rows.shape[0], dtype=jnp.int32)
    selector = (my_requests[:, None] == row_ids[None, :]).astype(jnp.bfloat16)
    own_cols = jnp.dot(selector, shard_rows, preferred_element_type=jnp.float32).astype(
        jnp.bfloat16
    )
    full_rows = lax.all_gather(own_cols, "head", axis=1, tiled=True)
    resident = full_rows.astype(jnp.float32)
    normed_attn = layer_norm(resident, ln1_gain, ln1_shift).astype(jnp.bfloat16)
    normed_mlp = layer_norm(resident, ln2_gain, ln2_shift).astype(jnp.bfloat16)
    projected = jnp.dot(
        normed_attn,
        w_qkv.reshape(w_qkv.shape[0], 3 * part_width),
        preferred_element_type=jnp.float32,
    )
    projected = projected.reshape(slot_rows, 3, part_width) + b_qkv[None]
    request_ids = jnp.arange(request_count, dtype=jnp.int32)
    my_lengths = jnp.sum(
        jnp.where(my_requests[:, None] == request_ids[None, :], lengths[None, :], 0), axis=1
    )
    queries = rotary(projected[:, 0].reshape(slot_rows, heads_here, HD), my_lengths).astype(
        jnp.bfloat16
    )
    new_keys = rotary(projected[:, 1].reshape(slot_rows, heads_here, HD), my_lengths).astype(
        jnp.bfloat16
    )
    new_values = projected[:, 2].reshape(slot_rows, heads_here, HD).astype(jnp.bfloat16)
    long_hits = my_requests[:, None] == jnp.arange(LONGS, dtype=jnp.int32)[None, :]
    long_part = jnp.sum(
        jnp.where(long_hits[:, :, None, None], queries.astype(jnp.float32)[:, None], 0.0), axis=0
    )
    long_queries = lax.psum(long_part, "seq")
    short_max = keys_short.shape[1]
    short_usable = (jnp.arange(short_max, dtype=jnp.int32)[None, :] < my_lengths[:, None]) & (
        my_lengths <= short_max
    )[:, None]
    short_keys = keys_short.reshape(slot_rows, short_max, heads_here, HD)
    short_vals = values_short.reshape(slot_rows, short_max, heads_here, HD)
    short_top, short_total, short_out = attend(queries, short_keys, short_vals, short_usable)
    own_score = jnp.sum(
        queries.astype(jnp.float32) * new_keys.astype(jnp.float32), axis=-1
    ) * HD ** (-0.5)
    piece_count = seq_count // LONGS
    my_piece = lax.dynamic_slice_in_dim(piece_map, seq_place, 1)[0]
    long_owner = my_piece // piece_count
    piece_index = my_piece % piece_count
    long_pick = jnp.arange(LONGS, dtype=jnp.int32) == long_owner
    piece_query = jnp.sum(jnp.where(long_pick[:, None, None], long_queries, 0.0), axis=0).astype(
        jnp.bfloat16
    )
    long_length = jnp.sum(jnp.where(long_pick, lengths[:LONGS], 0))
    piece_len = keys_long.shape[0]
    positions = piece_index * piece_len + jnp.arange(piece_len, dtype=jnp.int32)
    piece_usable = (positions < long_length)[None, :]
    piece_keys = keys_long.reshape(1, piece_len, heads_here, HD)
    piece_vals = values_long.reshape(1, piece_len, heads_here, HD)
    piece_top, piece_total, piece_out = attend(
        piece_query[None], piece_keys, piece_vals, piece_usable
    )
    spread_top = jnp.where(long_pick[:, None], piece_top, very_low)
    spread_total = jnp.where(long_pick[:, None], piece_total, 0.0)
    spread_out = jnp.where(long_pick[:, None, None], piece_out, 0.0)
    long_top, long_total, long_out = merged(
        (spread_top, spread_total, spread_out), "seq", combine_partials
    )
    has_long = jnp.any(long_hits, axis=1)
    mine_top = jnp.where(
        has_long[:, None],
        jnp.sum(jnp.where(long_hits[:, :, None], long_top[None], 0.0), axis=1),
        very_low,
    )
    mine_total = jnp.sum(jnp.where(long_hits[:, :, None], long_total[None], 0.0), axis=1)
    mine_out = jnp.sum(jnp.where(long_hits[:, :, None, None], long_out[None], 0.0), axis=1)
    summit = jnp.maximum(jnp.maximum(short_top, own_score), mine_top)
    short_scale = jnp.exp(short_top - summit)
    own_scale = jnp.exp(own_score - summit)
    long_scale = jnp.exp(mine_top - summit)
    denominator = short_total * short_scale + own_scale + mine_total * long_scale
    numerator = (
        short_out * short_scale[..., None]
        + new_values.astype(jnp.float32) * own_scale[..., None]
        + mine_out * long_scale[..., None]
    )
    attended = (
        (numerator / denominator[..., None]).reshape(slot_rows, part_width).astype(jnp.bfloat16)
    )
    hidden_units = jax.nn.gelu(
        jnp.dot(normed_mlp, w_up, preferred_element_type=jnp.float32) + b_up, approximate=False
    ).astype(jnp.bfloat16)
    partial_sum = jnp.dot(attended, w_dense, preferred_element_type=jnp.float32) + jnp.dot(
        hidden_units, w_down, preferred_element_type=jnp.float32
    )
    head_total = lax.psum_scatter(
        partial_sum.astype(jnp.bfloat16), "head", scatter_dimension=1, tiled=True
    ).astype(jnp.float32)
    finished = (own_cols.astype(jnp.float32) + head_total + b_dense + b_down).astype(jnp.bfloat16)
    home_ids = seq_place * slot_rows + jnp.arange(slot_rows, dtype=jnp.int32)
    selector = (slot_request[None, :] == home_ids[:, None]).astype(jnp.bfloat16)
    return jnp.dot(
        selector,
        lax.all_gather(finished, "seq", axis=0, tiled=True),
        preferred_element_type=jnp.float32,
    ).astype(jnp.bfloat16)


def solution(mesh):
    in_specs = (
        P("seq", "head"),
        P(),
        P(),
        P(),
        P(),
        P(None, None, "head"),
        P(None, "head"),
        P("head", None),
        P("head"),
        P(None, "head"),
        P("head"),
        P("head", None),
        P("head"),
        P("seq", None, "head"),
        P("seq", None, "head"),
        P("seq", "head"),
        P("seq", "head"),
        P(),
        P(),
        P(),
    )
    out_specs = P("seq", "head")
    return jax.shard_map(local, mesh=mesh, in_specs=in_specs, out_specs=out_specs, check_vma=False)
```

profile of v0, /device:TPU:0, one launch (start us, length us, event | category | flops | bytes accessed | tf_op | source)
XLA Modules:
  0.0 262.1 jit_solution(12537288334544157710)
XLA Ops:
  6.5 0.7 all-gather.3.cloned.1.call-update
  7.3 1.2 dynamic_slice.37
  11.2 17.0 %copy.30 = bf16[2048,3,1024]{0,2,1:T(8,128)(2,1)} copy(bf16[2048,3,1024]{2,0,1:T(8,128)(2,1)} %param.27) | data formatting | bytes 25165824 | tf_op args[5]
  28.2 0.1 dynamic_slice.36
  28.2 0.2 select_reduce_fusion.2
  28.5 6.5 %copy.47 = bf16[2048,1024]{0,1:T(8,128)(2,1)} copy(bf16[2048,1024]{1,0:T(8,128)(2,1)} %param.37) | data formatting | bytes 8388608 | tf_op jit(solution)/shard_map/reshape.2
  35.0 0.6 select_reduce_fusion.6
  35.7 0.6 add_compare_fusion
  36.3 0.1 fusion.106
  36.3 0.1 multiply_cosine_fusion
  36.5 13.8 %all-gather.3.cloned.1.call-done = bf16[512,1024]{1,0:T(8,128)(2,1)} async-done(((bf16[32,1024]{1,0:T(8,128)(2,1)}), bf16[512,1024]{1,0:T(8,128)(2,1)}) %all-gather.3.cloned.1.call-update) | async-done | bytes 1048592 | tf_op jit(solution)/shard_map/all_gather | solution.py:104
  50.3 1.5 convolution_convert_fusion.1
  51.8 4.9 %all_gather.22 = bf16[32,2048]{1,0:T(8,128)(2,1)S(1)} all-gather(bf16[32,1024]{1,0:T(8,128)(2,1)S(1)} %convolution_convert_fusion.1), channel_id=1, replica_groups=mesh['seq'=16,'head'=2] {'head'}, dimensions={1}, use_global_device_ids=true | all-gather | bytes 196608 | tf_op jit(solution)/shard_map/all_gather | solution.py:110
  56.8 0.1 convert_reduce_fusion
  56.9 0.2 fusion.26
  57.2 8.5 %fusion.15 = f32[32,3,1024]{2,0,1:T(8,128)S(1)} fusion(bf16[2048,3,1024]{0,2,1:T(8,128)(2,1)} %copy.30, f32[3,1024]{1,0:T(4,128)S(1)} %copy-done.1, bf16[32,2048]{1,0:T(8,128)(2,1)S(1)} %all_gather.22, f32[2048]{0:T(1024)S(1)} %copy-done.5, f32[2048]{0:T(1024)S(1)} %copy-done.6, f32[32]{0:T(128)S(1)} %add_rsqrt_fusion, f32[32]{0:T(128)S(1)} %broadcast_multiply_fusion), kind=kOutput, calls=%fused_computation.22 | convolution fusion | flops 403144704 | bytes 13136128 | tf_op jit(solution)/shard_map/dot_general | solution.py:114
  65.7 0.1 reshape_squeeze.7
  65.9 0.1 slice.84
  66.0 0.1 slice.85
  66.1 0.2 subtract_convert_fusion.1
  66.2 0.3 multiply_reduce_fusion
  66.6 3.4 %fusion.11 = f32[32,4,1,64]{3,2,1,0:T(1,128)S(1)} fusion(bf16[32,8,4,8,256]{4,3,2,1,0:T(8,128)(2,1)} %bitcast.118, bf16[32,4,256,1]{2,1,0,3:T(4,128)(2,1)S(1)} %bitcast.115), kind=kOutput, calls=%fused_computation.16 | convolution fusion | flops 4194304 | bytes 4292608 | tf_op jit(solution)/shard_map/rhc,rthc->rht/dot_general | solution.py:49
  70.0 0.1 fusion.96
  70.1 0.2 fusion.97
  70.3 0.1 select_reduce_fusion.1
  70.4 58.4 %psum.7 = f32[4,4,256]{2,1,0:T(4,128)S(1)} all-reduce(f32[4,4,256]{2,1,0:T(4,128)S(1)} %select_reduce_fusion.1), channel_id=1, replica_groups=mesh['seq'=16,'head'=2] {'seq'}, use_global_device_ids=true, to_apply=%region_8.9 | all-reduce | flops 4096 | bytes 32768 | tf_op jit(solution)/shard_map/psum | solution.py:135
  128.8 0.1 select_reduce_fusion.3
  128.9 3.0 %fusion.108 = f32[4,1,2048]{2,1,0:T(1,128)S(1)} fusion(bf16[2048,4,256]{0,2,1:T(8,128)(2,1)} %bitcast.112, bf16[4,256,1]{1,0,2:T(4,128)(2,1)S(1)} %bitcast.116), kind=kOutput, calls=%fused_computation.149 | convolution fusion | flops 4194304 | bytes 4229120 | tf_op jit(solution)/shard_map/rhc,rthc->rht/dot_general | solution.py:49
  131.9 0.1 fusion.107
  132.0 0.2 fusion.105
  132.3 0.7 fusion.5
  132.9 0.1 broadcast_select_fusion
  133.0 17.8 %all_gather.25 = f32[16,4,4,256]{3,2,1,0:T(4,128)S(1)} all-gather(f32[1,4,4,256]{3,2,1,0:T(4,128)S(1)} %broadcast_select_fusion), channel_id=1, replica_groups=mesh['seq'=16,'head'=2] {'seq'}, dimensions={0}, use_global_device_ids=true | all-gather | bytes 278528 | tf_op jit(solution)/shard_map/all_gather | solution.py:14
  150.9 0.1 broadcast_select_fusion.1
  150.9 19.3 %all_gather.24 = f32[16,4,4]{2,1,0:T(4,128)S(1)} all-gather(f32[1,4,4]{2,1,0:T(4,128)S(1)} %get-tuple-element.228), channel_id=1, replica_groups=mesh['seq'=16,'head'=2] {'seq'}, dimensions={0}, use_global_device_ids=true | all-gather | bytes 1088 | tf_op jit(solution)/shard_map/all_gather | solution.py:14
  170.2 17.7 %all_gather.23 = f32[16,4,4]{2,1,0:T(4,128)S(1)} all-gather(f32[1,4,4]{2,1,0:T(4,128)S(1)} %get-tuple-element.229), channel_id=1, replica_groups=mesh['seq'=16,'head'=2] {'seq'}, dimensions={0}, use_global_device_ids=true | all-gather | bytes 1088 | tf_op jit(solution)/shard_map/all_gather | solution.py:14
  187.9 2.0 while.19
  187.9 0.1 fusion.154
  188.0 0.1 fusion.154
  188.1 0.1 fusion.154
  188.3 0.1 fusion.154
  188.4 0.1 fusion.154
  188.5 0.1 fusion.154
  188.7 0.1 fusion.154
  188.8 0.1 fusion.154
  188.9 0.1 fusion.154
  189.1 0.1 fusion.154
  189.2 0.1 fusion.154
  189.3 0.1 fusion.154
  189.5 0.1 fusion.154
  189.6 0.1 fusion.154
  189.7 0.1 fusion.154
  189.8 0.1 select_reduce_fusion
  189.9 0.1 copy.31
  190.1 3.0 %fusion.8 = f32[32,4,1,256]{3,2,1,0:T(1,128)S(1)} fusion(bf16[32,8,4,8,256]{4,3,2,1,0:T(8,128)(2,1)} %bitcast.113, bf16[32,4,64,1]{2,0,1,3:T(8,128)(2,1)S(1)} %get-tuple-element.218), kind=kOutput, calls=%fused_computation.13 | convolution fusion | flops 4194304 | bytes 4341760 | tf_op jit(solution)/shard_map/rht,rthc->rhc/dot_general | solution.py:56
  193.1 0.1 select_reduce_fusion.5
  193.2 0.1 fusion.93
  193.4 0.1 copy-done
  193.5 0.8 fusion.143
  194.4 10.0 %fusion.14 = bf16[32,2048]{1,0:T(8,128)(2,1)} fusion(f32[32,2048]{1,0:T(8,128)S(1)} %fusion.143, bf16[2048,2048]{1,0:T(8,128)(2,1)} %param.33, bf16[2048,2048]{1,0:T(8,128)(2,1)} %param.31, bf16[32,2048]{1,0:T(8,128)(2,1)S(1)} %all_gather.22, f32[2048]{0:T(1024)S(1)} %copy-done.2, f32[2048]{0:T(1024)S(1)} %copy-done.3, f32[2048]{0:T(1024)S(1)} %copy-done.4, ...), kind=kOutput, calls=%fused_computation.21 | convolution fusion | flops 541720576 | bytes 17326336 | tf_op jit(solution)/shard_map/dot_general | solution.py:193
  204.5 8.8 %reduce-scatter.2.cloned.1.call-done = bf16[32,1024]{1,0:T(8,128)(2,1)} async-done(((bf16[32,2048]{1,0:T(8,128)(2,1)}), bf16[32,1024]{1,0:T(8,128)(2,1)}) %reduce-scatter.2.cloned.1.call-update) | async-done | bytes 65552 | tf_op jit(solution)/shard_map/reduce_scatter | solution.py:196
  213.2 1.5 add_convert_fusion
  214.8 38.6 %all-gather.5.cloned.1.call-done = bf16[512,1024]{1,0:T(8,128)(2,1)} async-done(((bf16[32,1024]{1,0:T(8,128)(2,1)}), bf16[512,1024]{1,0:T(8,128)(2,1)}) %all-gather.5.cloned.1.call-update) | async-done | bytes 1048592 | tf_op jit(solution)/shard_map/all_gather | solution.py:204
  253.4 2.2 convolution_convert_fusion
  (62 shorter events, 0.9 us)
Async XLA Ops:
  6.5 43.8 %all-gather.3.cloned.1.call-start = ((), (), s32[]{:S(2)}) async-start(), calls=%async_computation.1 | async-start | bytes 1114112 | tf_op jit(solution)/shard_map/all_gather | solution.py:104
  7.3 206.0 %reduce-scatter.2.cloned.1.call-start = ((), (), s32[]{:S(2)}) async-start(), calls=%async_computation.2 | async-start | bytes 196608 | tf_op jit(solution)/shard_map/reduce_scatter | solution.py:196
  11.2 17.0 %copy-start.9 = (s32[512]{0:T(512)S(1)}, s32[512]{0:T(512)}, u32[]{:S(2)}) copy-start(s32[512]{0:T(512)} %param.40) | copy-start | bytes 6148
  11.2 17.1 %copy-start.10 = (s32[512]{0:T(512)S(1)}, s32[512]{0:T(512)}, u32[]{:S(2)}) copy-start(s32[512]{0:T(512)} %param.39) | copy-start | bytes 6148
  28.4 28.7 %copy-start.1 = (f32[3,1024]{1,0:T(4,128)S(1)}, f32[3,1024]{1,0:T(4,128)}, u32[]{:S(2)}) copy-start(f32[3,1024]{1,0:T(4,128)} %param.28) | copy-start | bytes 36868
  28.4 28.7 %copy-start.5 = (f32[2048]{0:T(1024)S(1)}, f32[2048]{0:T(1024)}, u32[]{:S(2)}) copy-start(f32[2048]{0:T(1024)} %param.24) | copy-start | bytes 24580
  28.5 28.7 %copy-start.6 = (f32[2048]{0:T(1024)S(1)}, f32[2048]{0:T(1024)}, u32[]{:S(2)}) copy-start(f32[2048]{0:T(1024)} %param.23) | copy-start | bytes 24580
  128.8 3.4 %copy-start.11 = (bf16[2048,1024]{1,0:T(8,128)(2,1)S(1)}, bf16[2048,1024]{1,0:T(8,128)(2,1)}, u32[]{:S(2)}) copy-start(bf16[2048,1024]{1,0:T(8,128)(2,1)} %param.38) | copy-start | bytes 12582916
  190.1 3.5 %copy-start = (bf16[1024,2048]{1,0:T(8,128)(2,1)S(1)}, bf16[1024,2048]{1,0:T(8,128)(2,1)}, u32[]{:S(2)}) copy-start(bf16[1024,2048]{1,0:T(8,128)(2,1)} %param.29) | copy-start | bytes 12582916
  190.1 4.3 %copy-start.2 = (f32[2048]{0:T(1024)S(1)}, f32[2048]{0:T(1024)}, u32[]{:S(2)}) copy-start(f32[2048]{0:T(1024)} %param.32) | copy-start | bytes 24580
  190.1 4.3 %copy-start.3 = (f32[2048]{0:T(1024)S(1)}, f32[2048]{0:T(1024)}, u32[]{:S(2)}) copy-start(f32[2048]{0:T(1024)} %param.26) | copy-start | bytes 24580
  190.1 4.3 %copy-start.4 = (f32[2048]{0:T(1024)S(1)}, f32[2048]{0:T(1024)}, u32[]{:S(2)}) copy-start(f32[2048]{0:T(1024)} %param.25) | copy-start | bytes 24580
  194.4 18.9 %copy-start.7 = (f32[1024]{0:T(1024)S(1)}, f32[1024]{0:T(1024)}, u32[]{:S(2)}) copy-start(f32[1024]{0:T(1024)} %param.34) | copy-start | bytes 12292
  194.4 18.8 %copy-start.8 = (f32[1024]{0:T(1024)S(1)}, f32[1024]{0:T(1024)}, u32[]{:S(2)}) copy-start(f32[1024]{0:T(1024)} %param.30) | copy-start | bytes 12292
  204.4 49.0 %all-gather.5.cloned.1.call-start = ((), (), s32[]{:S(2)}) async-start(), calls=%async_computation.3 | async-start | bytes 1114112 | tf_op jit(solution)/shard_map/all_gather | solution.py:204
Sparse Core Ops, SparseCore 0:
  9.5 40.7 all-gather.2
  204.5 8.6 reduce-scatter.1
  215.4 37.9 all-gather.4
where the time goes:
time: 263 us; the launch traced here: 262 us
  blocking collectives  118 us (45%)
  waiting for transfers between devices  61.9 us (24%)
  matrix products  33 us (13%)
  local copies, waits for them, and re-layouts  25.6 us (10%)
  between operations  16 us (6%)
  other arithmetic  7.06 us (3%)
    psum x1, blocking collectives, local(): long_queries = lax.psum(long_part, 'seq')  58.4 us
    all_gather x3, blocking collectives, merged(): everything = jax.tree.map(lambda part: lax.all_gather(part, axis), array)  54.8 us
    all_gather x1, waiting for transfers between devices, local(): lax.all_gather(finished, 'seq', axis=0, tiled=True)  38.6 us
    unnamed x25, local copies, waits for them, and re-layouts  17.2 us
    all_gather x1, waiting for transfers between devices, local(): shard_rows = lax.all_gather(tokens, 'seq', axis=0, tiled=True)  13.8 us
    dot_general x1, matrix products, local(): jnp.dot(hidden_units, w_down, preferred_element_type=jnp.float32)  9.99 us
    reduce_scatter x1, waiting for transfers between devices, local(): lax.psum_scatter(partial_sum.astype(jnp.bfloat16), 'head', scatter_dimens...  8.76 us
    dot_general x1, matrix products, local(): jnp.dot(normed_attn, w_qkv.reshape(w_qkv.shape[0], 3 * part_width), prefe...  8.47 us
  transfers between devices with their start and end apart: 3, of which 3 were waited for; matrix products, arithmetic and copies ran while one was open for 10% of the time, Pallas kernels for 0%

commit v1 on v0

--- a/solution.py
+++ b/solution.py
@@ -101,7 +101,23 @@
     request_count = slot_request.shape[0]
     heads_here = part_width // HD
     my_requests = lax.dynamic_slice_in_dim(slot_request, seq_place * slot_rows, slot_rows)
-    shard_rows = lax.all_gather(tokens, "seq", axis=0, tiled=True)
+    size, here, span = (lax.axis_size("seq"), lax.axis_index("seq"), tokens.shape[0])
+    forward = [(i, (i + 1) % size) for i in range(size)]
+    left = [(i, (i - 1) % size) for i in range(size)]
+    shard_rows = jnp.zeros((*tokens.shape[:0], size * span, *tokens.shape[0 + 1 :]), tokens.dtype)
+    shard_rows = lax.dynamic_update_slice_in_dim(shard_rows, tokens, here * span, axis=0)
+    from_left = from_right = tokens
+    halfway = size // 2
+    for step in range(1, halfway + 1):
+        from_left = lax.ppermute(from_left, "seq", forward)
+        shard_rows = lax.dynamic_update_slice_in_dim(
+            shard_rows, from_left, (here - step) % size * span, axis=0
+        )
+        if step < size - halfway:
+            from_right = lax.ppermute(from_right, "seq", left)
+            shard_rows = lax.dynamic_update_slice_in_dim(
+                shard_rows, from_right, (here + step) % size * span, axis=0
+            )
     row_ids = jnp.arange(shard_rows.shape[0], dtype=jnp.int32)
     selector = (my_requests[:, None] == row_ids[None, :]).astype(jnp.bfloat16)
     own_cols = jnp.dot(selector, shard_rows, preferred_element_type=jnp.float32).astype(

time: 263 us -> 301 us (1.14)
  starting transfers between devices: 0.08 us -> 32.4 us
  waiting for transfers between devices: 61.9 us -> 65.6 us
    ppermute x0 -> x15, starting transfers between devices: none -> 32.3 us  [the longest x7 31.8 us: local(): from_right = lax.ppermute(from_right, 'seq', left)]
    ppermute x0 -> x15, waiting for transfers between devices: none -> 17.7 us  [the longest x8 17.6 us: local(): from_left = lax.ppermute(from_left, 'seq', forward)]
    all_gather x1 -> x0, waiting for transfers between devices: 13.8 us -> none  [local(): shard_rows = lax.all_gather(tokens, 'seq', axis=0, tiled=True)]
    unnamed x25 -> x23, local copies, waits for them, and re-layouts: 17.2 us -> 17.2 us
  transfers between devices with their start and end apart: 3 -> 17, of which waited for: 3 -> 9; matrix products, arithmetic and copies ran while one was open for 10% -> 10% of each run, Pallas kernels for 0% -> 0%
where the time goes in v1:
time: 301 us; the launch traced here: 300 us
  blocking collectives  117 us (39%)
  waiting for transfers between devices  65.6 us (22%)
  starting transfers between devices  32.4 us (11%)
  matrix products  31.8 us (11%)
  local copies, waits for them, and re-layouts  27.4 us (9%)
  between operations  16.4 us (5%)
  other arithmetic  8.44 us (3%)
    psum x1, blocking collectives, local(): long_queries = lax.psum(long_part, 'seq')  57.6 us
    all_gather x3, blocking collectives, merged(): everything = jax.tree.map(lambda part: lax.all_gather(part, axis), array)  54.8 us
    all_gather x1, waiting for transfers between devices, local(): lax.all_gather(finished, 'seq', axis=0, tiled=True)  38.6 us
    ppermute x7, starting transfers between devices, local(): from_right = lax.ppermute(from_right, 'seq', left)  31.8 us
    ppermute x8, waiting for transfers between devices, local(): from_left = lax.ppermute(from_left, 'seq', forward)  17.6 us
    unnamed x23, local copies, waits for them, and re-layouts  17.2 us
    dot_general x1, matrix products, local(): jnp.dot(hidden_units, w_down, preferred_element_type=jnp.float32)  9.99 us
    reduce_scatter x1, waiting for transfers between devices, local(): lax.psum_scatter(partial_sum.astype(jnp.bfloat16), 'head', scatter_dimens...  9.23 us
  transfers between devices with their start and end apart: 17, of which 9 were waited for; matrix products, arithmetic and copies ran while one was open for 10% of the time, Pallas kernels for 0%

profile of v1, /device:TPU:0, one launch (start us, length us, event | category | flops | bytes accessed | tf_op | source)
XLA Modules:
  0.0 299.5 jit_solution(9034793276446551878)
XLA Ops:
  6.5 0.5 collective-permute-start
  7.0 5.0 %collective-permute-start.1 = (bf16[32,1024]{1,0:T(8,128)(2,1)}, bf16[32,1024]{1,0:T(8,128)(2,1)S(1)}, u32[]{:S(2)}, u32[]{:S(2)}) collective-permute-start(bf16[32,1024]{1,0:T(8,128)(2,1)} %param.22), channel_id=1, source_target_pairs={{0,30},{2,0},{4,2},{6,4},{8,6},{10,8},{12,10},{14,12},{16,14},{18,... | collective-permute-start | bytes 196616 | tf_op jit(solution)/shard_map/ppermute | solution.py:117
  12.0 0.8 dynamic_slice.36
  12.8 0.9 select_reduce_fusion.2
  13.7 1.2 dynamic_slice.37
  17.5 0.1 broadcast_in_dim.255
  17.6 0.9 constant_dynamic-update-slice_fusion.15
  18.5 17.0 %copy.30 = bf16[2048,3,1024]{0,2,1:T(8,128)(2,1)} copy(bf16[2048,3,1024]{2,0,1:T(8,128)(2,1)} %param.27) | data formatting | bytes 25165824 | tf_op args[5]
  35.5 6.5 %copy.47 = bf16[2048,1024]{0,1:T(8,128)(2,1)} copy(bf16[2048,1024]{1,0:T(8,128)(2,1)} %param.37) | data formatting | bytes 8388608 | tf_op jit(solution)/shard_map/reshape.2
  42.1 1.3 select_reduce_fusion.6
  43.4 0.1 multiply_cosine_fusion
  43.5 0.6 add_compare_fusion
  44.2 4.4 %collective-permute-start.3 = (bf16[32,1024]{1,0:T(8,128)(2,1)S(1)}, bf16[32,1024]{1,0:T(8,128)(2,1)S(1)}, u32[]{:S(2)}, u32[]{:S(2)}) collective-permute-start(bf16[32,1024]{1,0:T(8,128)(2,1)S(1)} %collective-permute-done.1), channel_id=1, source_target_pairs={{0,30},{2,0},{4,2},{6,4},{8,6},{10,8},{12,10},{14,12},{16,14},{18,... | collective-permute-start | bytes 196616 | tf_op jit(solution)/shard_map/ppermute | solution.py:117
  48.7 1.9 collective-permute-done.2
  50.6 4.4 %collective-permute-start.5 = (bf16[32,1024]{1,0:T(8,128)(2,1)S(1)}, bf16[32,1024]{1,0:T(8,128)(2,1)S(1)}, u32[]{:S(2)}, u32[]{:S(2)}) collective-permute-start(bf16[32,1024]{1,0:T(8,128)(2,1)S(1)} %collective-permute-done.3), channel_id=1, source_target_pairs={{0,30},{2,0},{4,2},{6,4},{8,6},{10,8},{12,10},{14,12},{16,14},{18,... | collective-permute-start | bytes 196616 | tf_op jit(solution)/shard_map/ppermute | solution.py:117
  55.1 1.9 collective-permute-done.4
  57.0 4.5 %collective-permute-start.7 = (bf16[32,1024]{1,0:T(8,128)(2,1)S(1)}, bf16[32,1024]{1,0:T(8,128)(2,1)S(1)}, u32[]{:S(2)}, u32[]{:S(2)}) collective-permute-start(bf16[32,1024]{1,0:T(8,128)(2,1)S(1)} %collective-permute-done.5), channel_id=1, source_target_pairs={{0,30},{2,0},{4,2},{6,4},{8,6},{10,8},{12,10},{14,12},{16,14},{18,... | collective-permute-start | bytes 196616 | tf_op jit(solution)/shard_map/ppermute | solution.py:117
  61.5 1.9 collective-permute-done.6
  63.4 4.5 %collective-permute-start.9 = (bf16[32,1024]{1,0:T(8,128)(2,1)S(1)}, bf16[32,1024]{1,0:T(8,128)(2,1)S(1)}, u32[]{:S(2)}, u32[]{:S(2)}) collective-permute-start(bf16[32,1024]{1,0:T(8,128)(2,1)S(1)} %collective-permute-done.7), channel_id=1, source_target_pairs={{0,30},{2,0},{4,2},{6,4},{8,6},{10,8},{12,10},{14,12},{16,14},{18,... | collective-permute-start | bytes 196616 | tf_op jit(solution)/shard_map/ppermute | solution.py:117
  67.9 1.9 collective-permute-done.8
  69.8 4.5 %collective-permute-start.11 = (bf16[32,1024]{1,0:T(8,128)(2,1)S(1)}, bf16[32,1024]{1,0:T(8,128)(2,1)S(1)}, u32[]{:S(2)}, u32[]{:S(2)}) collective-permute-start(bf16[32,1024]{1,0:T(8,128)(2,1)S(1)} %collective-permute-done.9), channel_id=1, source_target_pairs={{0,30},{2,0},{4,2},{6,4},{8,6},{10,8},{12,10},{14,12},{16,14},{18,... | collective-permute-start | bytes 196616 | tf_op jit(solution)/shard_map/ppermute | solution.py:117
  74.3 1.9 collective-permute-done.10
  76.2 4.5 %collective-permute-start.13 = (bf16[32,1024]{1,0:T(8,128)(2,1)S(1)}, bf16[32,1024]{1,0:T(8,128)(2,1)S(1)}, u32[]{:S(2)}, u32[]{:S(2)}) collective-permute-start(bf16[32,1024]{1,0:T(8,128)(2,1)S(1)} %collective-permute-done.11), channel_id=1, source_target_pairs={{0,30},{2,0},{4,2},{6,4},{8,6},{10,8},{12,10},{14,12},{16,14},{18,... | collective-permute-start | bytes 196616 | tf_op jit(solution)/shard_map/ppermute | solution.py:117
  80.7 1.9 collective-permute-done.12
  82.6 6.3 %collective-permute-done.14 = bf16[32,1024]{1,0:T(8,128)(2,1)S(1)} collective-permute-done((bf16[32,1024]{1,0:T(8,128)(2,1)S(1)}, bf16[32,1024]{1,0:T(8,128)(2,1)S(1)}, u32[]{:S(2)}, u32[]{:S(2)}) %collective-permute-start.14) | collective-permute-done | bytes 65568 | tf_op jit(solution)/shard_map/ppermute | solution.py:112
  88.9 0.3 convolution_convert_fusion.1
  89.2 4.9 %all_gather.18 = bf16[32,2048]{1,0:T(8,128)(2,1)S(1)} all-gather(bf16[32,1024]{1,0:T(8,128)(2,1)S(1)} %convolution_convert_fusion.1), channel_id=1, replica_groups=mesh['seq'=16,'head'=2] {'head'}, dimensions={1}, use_global_device_ids=true | all-gather | bytes 196608 | tf_op jit(solution)/shard_map/all_gather | solution.py:126
  94.2 0.1 convert_reduce_fusion
  94.3 0.2 fusion.26
  94.6 8.5 %fusion.15 = f32[32,3,1024]{2,0,1:T(8,128)S(1)} fusion(bf16[2048,3,1024]{0,2,1:T(8,128)(2,1)} %copy.30, f32[3,1024]{1,0:T(4,128)S(1)} %copy-done.1, bf16[32,2048]{1,0:T(8,128)(2,1)S(1)} %all_gather.18, f32[2048]{0:T(1024)S(1)} %copy-done.5, f32[2048]{0:T(1024)S(1)} %copy-done.6, f32[32]{0:T(128)S(1)} %add_rsqrt_fusion, f32[32]{0:T(128)S(1)} %broadcast_multiply_fusion), kind=kOutput, calls=%fused_computation.22 | convolution fusion | flops 403144704 | bytes 13136128 | tf_op jit(solution)/shard_map/dot_general | solution.py:130
  103.3 0.1 slice.84
  103.4 0.1 slice.85
  103.5 0.2 subtract_convert_fusion.1
  103.6 0.3 multiply_reduce_fusion
  104.0 3.4 %fusion.11 = f32[32,4,1,64]{3,2,1,0:T(1,128)S(1)} fusion(bf16[32,8,4,8,256]{4,3,2,1,0:T(8,128)(2,1)} %bitcast.118, bf16[32,4,256,1]{2,1,0,3:T(4,128)(2,1)S(1)} %bitcast.115), kind=kOutput, calls=%fused_computation.16 | convolution fusion | flops 4194304 | bytes 4292608 | tf_op jit(solution)/shard_map/rhc,rthc->rht/dot_general | solution.py:49
  107.4 0.1 fusion.96
  107.5 0.2 fusion.97
  107.6 0.1 select_reduce_fusion.1
  107.8 57.6 %psum.7 = f32[4,4,256]{2,1,0:T(4,128)S(1)} all-reduce(f32[4,4,256]{2,1,0:T(4,128)S(1)} %select_reduce_fusion.1), channel_id=1, replica_groups=mesh['seq'=16,'head'=2] {'seq'}, use_global_device_ids=true, to_apply=%region_8.9 | all-reduce | flops 4096 | bytes 32768 | tf_op jit(solution)/shard_map/psum | solution.py:151
  165.5 3.0 fusion.108
  168.5 0.1 fusion.107
  168.6 0.2 fusion.105
  168.9 0.6 fusion.5
  169.6 17.8 %all_gather.21 = f32[16,4,4,256]{3,2,1,0:T(4,128)S(1)} all-gather(f32[1,4,4,256]{3,2,1,0:T(4,128)S(1)} %broadcast_select_fusion), channel_id=1, replica_groups=mesh['seq'=16,'head'=2] {'seq'}, dimensions={0}, use_global_device_ids=true | all-gather | bytes 278528 | tf_op jit(solution)/shard_map/all_gather | solution.py:14
  187.5 19.3 %all_gather.20 = f32[16,4,4]{2,1,0:T(4,128)S(1)} all-gather(f32[1,4,4]{2,1,0:T(4,128)S(1)} %get-tuple-element.228), channel_id=1, replica_groups=mesh['seq'=16,'head'=2] {'seq'}, dimensions={0}, use_global_device_ids=true | all-gather | bytes 1088 | tf_op jit(solution)/shard_map/all_gather | solution.py:14
  206.8 17.7 %all_gather.19 = f32[16,4,4]{2,1,0:T(4,128)S(1)} all-gather(f32[1,4,4]{2,1,0:T(4,128)S(1)} %get-tuple-element.229), channel_id=1, replica_groups=mesh['seq'=16,'head'=2] {'seq'}, dimensions={0}, use_global_device_ids=true | all-gather | bytes 1088 | tf_op jit(solution)/shard_map/all_gather | solution.py:14
  224.4 2.0 while.19
  224.6 0.1 fusion.154
  224.9 0.1 fusion.154
  225.1 0.1 fusion.154
  225.4 0.1 fusion.154
  225.7 0.1 fusion.154
  225.9 0.1 fusion.154
  226.2 0.1 fusion.154
  226.4 0.1 select_reduce_fusion
  226.7 3.0 %fusion.8 = f32[32,4,1,256]{3,2,1,0:T(1,128)S(1)} fusion(bf16[32,8,4,8,256]{4,3,2,1,0:T(8,128)(2,1)} %bitcast.113, bf16[32,4,64,1]{2,0,1,3:T(8,128)(2,1)S(1)} %get-tuple-element.218), kind=kOutput, calls=%fused_computation.13 | convolution fusion | flops 4194304 | bytes 4341760 | tf_op jit(solution)/shard_map/rht,rthc->rhc/dot_general | solution.py:56
  229.8 0.1 fusion.93
  230.0 0.1 copy-done
  230.1 0.8 fusion.143
  231.0 10.0 %fusion.14 = bf16[32,2048]{1,0:T(8,128)(2,1)} fusion(f32[32,2048]{1,0:T(8,128)S(1)} %fusion.143, bf16[2048,2048]{1,0:T(8,128)(2,1)} %param.33, bf16[2048,2048]{1,0:T(8,128)(2,1)} %param.31, bf16[32,2048]{1,0:T(8,128)(2,1)S(1)} %all_gather.18, f32[2048]{0:T(1024)S(1)} %copy-done.2, f32[2048]{0:T(1024)S(1)} %copy-done.3, f32[2048]{0:T(1024)S(1)} %copy-done.4, ...), kind=kOutput, calls=%fused_computation.21 | convolution fusion | flops 541720576 | bytes 17326336 | tf_op jit(solution)/shard_map/dot_general | solution.py:209
  241.1 9.2 %reduce-scatter.2.cloned.1.call-done = bf16[32,1024]{1,0:T(8,128)(2,1)} async-done(((bf16[32,2048]{1,0:T(8,128)(2,1)}), bf16[32,1024]{1,0:T(8,128)(2,1)}) %reduce-scatter.2.cloned.1.call-update) | async-done | bytes 65552 | tf_op jit(solution)/shard_map/reduce_scatter | solution.py:212
  250.3 1.5 add_convert_fusion
  251.9 38.6 %all-gather.2.cloned.1.call-done = bf16[512,1024]{1,0:T(8,128)(2,1)} async-done(((bf16[32,1024]{1,0:T(8,128)(2,1)}), bf16[512,1024]{1,0:T(8,128)(2,1)}) %all-gather.2.cloned.1.call-update) | async-done | bytes 1048592 | tf_op jit(solution)/shard_map/all_gather | solution.py:220
  290.5 2.2 convolution_convert_fusion
  (104 shorter events, 2.4 us)
Async XLA Ops:
  6.5 243.8 %reduce-scatter.2.cloned.1.call-start = ((), (), s32[]{:S(2)}) async-start(), calls=%async_computation.1 | async-start | bytes 196608 | tf_op jit(solution)/shard_map/reduce_scatter | solution.py:212
  6.5 37.6 %collective-permute-start = (bf16[32,1024]{1,0:T(8,128)(2,1)}, bf16[32,1024]{1,0:T(8,128)(2,1)S(1)}, u32[]{:S(2)}, u32[]{:S(2)}) collective-permute-start(bf16[32,1024]{1,0:T(8,128)(2,1)} %param.22), channel_id=1, source_target_pairs={{0,2},{2,4},{4,6},{6,8},{8,10},{10,12},{12,14},{14,16},{16,18},{18... | collective-permute-start | bytes 196616 | tf_op jit(solution)/shard_map/ppermute | solution.py:112
  7.0 37.2 %collective-permute-start.1 = (bf16[32,1024]{1,0:T(8,128)(2,1)}, bf16[32,1024]{1,0:T(8,128)(2,1)S(1)}, u32[]{:S(2)}, u32[]{:S(2)}) collective-permute-start(bf16[32,1024]{1,0:T(8,128)(2,1)} %param.22), channel_id=1, source_target_pairs={{0,30},{2,0},{4,2},{6,4},{8,6},{10,8},{12,10},{14,12},{16,14},{18,... | collective-permute-start | bytes 196616 | tf_op jit(solution)/shard_map/ppermute | solution.py:117
  35.5 59.0 %copy-start.1 = (f32[3,1024]{1,0:T(4,128)S(1)}, f32[3,1024]{1,0:T(4,128)}, u32[]{:S(2)}) copy-start(f32[3,1024]{1,0:T(4,128)} %param.28) | copy-start | bytes 36868
  35.5 59.0 %copy-start.5 = (f32[2048]{0:T(1024)S(1)}, f32[2048]{0:T(1024)}, u32[]{:S(2)}) copy-start(f32[2048]{0:T(1024)} %param.24) | copy-start | bytes 24580
  35.5 59.1 %copy-start.6 = (f32[2048]{0:T(1024)S(1)}, f32[2048]{0:T(1024)}, u32[]{:S(2)}) copy-start(f32[2048]{0:T(1024)} %param.23) | copy-start | bytes 24580
  44.1 6.5 %collective-permute-start.2 = (bf16[32,1024]{1,0:T(8,128)(2,1)S(1)}, bf16[32,1024]{1,0:T(8,128)(2,1)S(1)}, u32[]{:S(2)}, u32[]{:S(2)}) collective-permute-start(bf16[32,1024]{1,0:T(8,128)(2,1)S(1)} %collective-permute-done), channel_id=1, source_target_pairs={{0,2},{2,4},{4,6},{6,8},{8,10},{10,12},{12,14},{14,16},{16,18},{18... | collective-permute-start | bytes 196616 | tf_op jit(solution)/shard_map/ppermute | solution.py:112
  44.2 6.4 %collective-permute-start.3 = (bf16[32,1024]{1,0:T(8,128)(2,1)S(1)}, bf16[32,1024]{1,0:T(8,128)(2,1)S(1)}, u32[]{:S(2)}, u32[]{:S(2)}) collective-permute-start(bf16[32,1024]{1,0:T(8,128)(2,1)S(1)} %collective-permute-done.1), channel_id=1, source_target_pairs={{0,30},{2,0},{4,2},{6,4},{8,6},{10,8},{12,10},{14,12},{16,14},{18,... | collective-permute-start | bytes 196616 | tf_op jit(solution)/shard_map/ppermute | solution.py:117
  50.6 6.4 %collective-permute-start.4 = (bf16[32,1024]{1,0:T(8,128)(2,1)S(1)}, bf16[32,1024]{1,0:T(8,128)(2,1)S(1)}, u32[]{:S(2)}, u32[]{:S(2)}) collective-permute-start(bf16[32,1024]{1,0:T(8,128)(2,1)S(1)} %collective-permute-done.2), channel_id=1, source_target_pairs={{0,2},{2,4},{4,6},{6,8},{8,10},{10,12},{12,14},{14,16},{16,18},{18... | collective-permute-start | bytes 196616 | tf_op jit(solution)/shard_map/ppermute | solution.py:112
  50.6 6.4 %collective-permute-start.5 = (bf16[32,1024]{1,0:T(8,128)(2,1)S(1)}, bf16[32,1024]{1,0:T(8,128)(2,1)S(1)}, u32[]{:S(2)}, u32[]{:S(2)}) collective-permute-start(bf16[32,1024]{1,0:T(8,128)(2,1)S(1)} %collective-permute-done.3), channel_id=1, source_target_pairs={{0,30},{2,0},{4,2},{6,4},{8,6},{10,8},{12,10},{14,12},{16,14},{18,... | collective-permute-start | bytes 196616 | tf_op jit(solution)/shard_map/ppermute | solution.py:117
  57.0 6.4 %collective-permute-start.6 = (bf16[32,1024]{1,0:T(8,128)(2,1)S(1)}, bf16[32,1024]{1,0:T(8,128)(2,1)S(1)}, u32[]{:S(2)}, u32[]{:S(2)}) collective-permute-start(bf16[32,1024]{1,0:T(8,128)(2,1)S(1)} %collective-permute-done.4), channel_id=1, source_target_pairs={{0,2},{2,4},{4,6},{6,8},{8,10},{10,12},{12,14},{14,16},{16,18},{18... | collective-permute-start | bytes 196616 | tf_op jit(solution)/shard_map/ppermute | solution.py:112
  57.0 6.4 %collective-permute-start.7 = (bf16[32,1024]{1,0:T(8,128)(2,1)S(1)}, bf16[32,1024]{1,0:T(8,128)(2,1)S(1)}, u32[]{:S(2)}, u32[]{:S(2)}) collective-permute-start(bf16[32,1024]{1,0:T(8,128)(2,1)S(1)} %collective-permute-done.5), channel_id=1, source_target_pairs={{0,30},{2,0},{4,2},{6,4},{8,6},{10,8},{12,10},{14,12},{16,14},{18,... | collective-permute-start | bytes 196616 | tf_op jit(solution)/shard_map/ppermute | solution.py:117
  63.4 6.4 %collective-permute-start.8 = (bf16[32,1024]{1,0:T(8,128)(2,1)S(1)}, bf16[32,1024]{1,0:T(8,128)(2,1)S(1)}, u32[]{:S(2)}, u32[]{:S(2)}) collective-permute-start(bf16[32,1024]{1,0:T(8,128)(2,1)S(1)} %collective-permute-done.6), channel_id=1, source_target_pairs={{0,2},{2,4},{4,6},{6,8},{8,10},{10,12},{12,14},{14,16},{16,18},{18... | collective-permute-start | bytes 196616 | tf_op jit(solution)/shard_map/ppermute | solution.py:112
  63.4 6.4 %collective-permute-start.9 = (bf16[32,1024]{1,0:T(8,128)(2,1)S(1)}, bf16[32,1024]{1,0:T(8,128)(2,1)S(1)}, u32[]{:S(2)}, u32[]{:S(2)}) collective-permute-start(bf16[32,1024]{1,0:T(8,128)(2,1)S(1)} %collective-permute-done.7), channel_id=1, source_target_pairs={{0,30},{2,0},{4,2},{6,4},{8,6},{10,8},{12,10},{14,12},{16,14},{18,... | collective-permute-start | bytes 196616 | tf_op jit(solution)/shard_map/ppermute | solution.py:117
  69.8 6.4 %collective-permute-start.10 = (bf16[32,1024]{1,0:T(8,128)(2,1)S(1)}, bf16[32,1024]{1,0:T(8,128)(2,1)S(1)}, u32[]{:S(2)}, u32[]{:S(2)}) collective-permute-start(bf16[32,1024]{1,0:T(8,128)(2,1)S(1)} %collective-permute-done.8), channel_id=1, source_target_pairs={{0,2},{2,4},{4,6},{6,8},{8,10},{10,12},{12,14},{14,16},{16,18},{18... | collective-permute-start | bytes 196616 | tf_op jit(solution)/shard_map/ppermute | solution.py:112
  69.8 6.4 %collective-permute-start.11 = (bf16[32,1024]{1,0:T(8,128)(2,1)S(1)}, bf16[32,1024]{1,0:T(8,128)(2,1)S(1)}, u32[]{:S(2)}, u32[]{:S(2)}) collective-permute-start(bf16[32,1024]{1,0:T(8,128)(2,1)S(1)} %collective-permute-done.9), channel_id=1, source_target_pairs={{0,30},{2,0},{4,2},{6,4},{8,6},{10,8},{12,10},{14,12},{16,14},{18,... | collective-permute-start | bytes 196616 | tf_op jit(solution)/shard_map/ppermute | solution.py:117
  76.1 6.4 %collective-permute-start.12 = (bf16[32,1024]{1,0:T(8,128)(2,1)S(1)}, bf16[32,1024]{1,0:T(8,128)(2,1)S(1)}, u32[]{:S(2)}, u32[]{:S(2)}) collective-permute-start(bf16[32,1024]{1,0:T(8,128)(2,1)S(1)} %collective-permute-done.10), channel_id=1, source_target_pairs={{0,2},{2,4},{4,6},{6,8},{8,10},{10,12},{12,14},{14,16},{16,18},{18... | collective-permute-start | bytes 196616 | tf_op jit(solution)/shard_map/ppermute | solution.py:112
  76.2 6.4 %collective-permute-start.13 = (bf16[32,1024]{1,0:T(8,128)(2,1)S(1)}, bf16[32,1024]{1,0:T(8,128)(2,1)S(1)}, u32[]{:S(2)}, u32[]{:S(2)}) collective-permute-start(bf16[32,1024]{1,0:T(8,128)(2,1)S(1)} %collective-permute-done.11), channel_id=1, source_target_pairs={{0,30},{2,0},{4,2},{6,4},{8,6},{10,8},{12,10},{14,12},{16,14},{18,... | collective-permute-start | bytes 196616 | tf_op jit(solution)/shard_map/ppermute | solution.py:117
  82.5 6.4 %collective-permute-start.14 = (bf16[32,1024]{1,0:T(8,128)(2,1)S(1)}, bf16[32,1024]{1,0:T(8,128)(2,1)S(1)}, u32[]{:S(2)}, u32[]{:S(2)}) collective-permute-start(bf16[32,1024]{1,0:T(8,128)(2,1)S(1)} %collective-permute-done.12), channel_id=1, source_target_pairs={{0,2},{2,4},{4,6},{6,8},{8,10},{10,12},{12,14},{14,16},{16,18},{18... | collective-permute-start | bytes 196616 | tf_op jit(solution)/shard_map/ppermute | solution.py:112
  165.4 3.4 %copy-start.10 = (bf16[2048,1024]{1,0:T(8,128)(2,1)S(1)}, bf16[2048,1024]{1,0:T(8,128)(2,1)}, u32[]{:S(2)}) copy-start(bf16[2048,1024]{1,0:T(8,128)(2,1)} %param.38) | copy-start | bytes 12582916
  226.7 3.5 %copy-start = (bf16[1024,2048]{1,0:T(8,128)(2,1)S(1)}, bf16[1024,2048]{1,0:T(8,128)(2,1)}, u32[]{:S(2)}) copy-start(bf16[1024,2048]{1,0:T(8,128)(2,1)} %param.29) | copy-start | bytes 12582916
  226.7 4.3 %copy-start.2 = (f32[2048]{0:T(1024)S(1)}, f32[2048]{0:T(1024)}, u32[]{:S(2)}) copy-start(f32[2048]{0:T(1024)} %param.32) | copy-start | bytes 24580
  226.7 4.3 %copy-start.3 = (f32[2048]{0:T(1024)S(1)}, f32[2048]{0:T(1024)}, u32[]{:S(2)}) copy-start(f32[2048]{0:T(1024)} %param.26) | copy-start | bytes 24580
  226.7 4.3 %copy-start.4 = (f32[2048]{0:T(1024)S(1)}, f32[2048]{0:T(1024)}, u32[]{:S(2)}) copy-start(f32[2048]{0:T(1024)} %param.25) | copy-start | bytes 24580
  231.0 19.3 %copy-start.7 = (f32[1024]{0:T(1024)S(1)}, f32[1024]{0:T(1024)}, u32[]{:S(2)}) copy-start(f32[1024]{0:T(1024)} %param.34) | copy-start | bytes 12292
  231.0 19.3 %copy-start.8 = (f32[1024]{0:T(1024)S(1)}, f32[1024]{0:T(1024)}, u32[]{:S(2)}) copy-start(f32[1024]{0:T(1024)} %param.30) | copy-start | bytes 12292
  231.0 59.5 %copy-start.9 = (s32[512]{0:T(512)S(1)}, s32[512]{0:T(512)}, u32[]{:S(2)}) copy-start(s32[512]{0:T(512)} %param.40) | copy-start | bytes 6148
  241.1 49.5 %all-gather.2.cloned.1.call-start = ((), (), s32[]{:S(2)}) async-start(), calls=%async_computation.2 | async-start | bytes 1114112 | tf_op jit(solution)/shard_map/all_gather | solution.py:220
Sparse Core Ops, SparseCore 0:
  241.2 9.1 reduce-scatter.1
  252.5 37.9 all-gather.1
